TPU v7x, 128 devices: a whole 4x4x4 slice. The times are simulated.
128 devices in a mesh: dp: 8 (over y, x_lo), mp: 16 (over x_hi, z, core).
Axes of the slice: x: 4 (x_hi: 2, x_lo: 2; x = x_hi * 2 + x_lo), y: 4, z: 4, core: 2. Of those that a mesh axis runs over, the one named last changes fastest.
Arguments:
- hidden_states: bfloat16 [4096, 4096], P('dp', 'mp'), may hold values from -6 to 6
- gate_online: bfloat16 [4096, 14336], P('dp', 'mp'), may hold values from -0.09375 to 0.09375
- up_online: bfloat16 [4096, 14336], P('dp', 'mp'), may hold values from -0.09375 to 0.09375
- down_online: bfloat16 [14336, 4096], P('mp', 'dp'), may hold values from -0.046875 to 0.046875
- gate_previous: bfloat16 [4096, 14336], P(None, 'mp'), may hold values from -0.09375 to 0.09375
- up_previous: bfloat16 [4096, 14336], P(None, 'mp'), may hold values from -0.09375 to 0.09375
- down_previous: bfloat16 [14336, 4096], P('mp'), may hold values from -0.046875 to 0.046875
Outputs:
- online_output: bfloat16 [4096, 4096], P('dp', 'mp')
- target_output: bfloat16 [4096, 4096], P('dp', 'mp')
All inputs are finite; a program needn't handle non-finite values.
Results may differ from a plain program's by a relative error of at most 0.0072.
Values may be sent and summed in bfloat16 or wider, within the bound.
A program may use at most 128 MiB of HBM per device.

v0:
```python
import jax
import jax.numpy as jnp
from jax import lax
from jax.sharding import PartitionSpec as P

POLYAK = 0.25


def blend(online, previous):
    return (
        POLYAK * online.astype(jnp.float32) + (1.0 - POLYAK) * previous.astype(jnp.float32)
    ).astype(jnp.bfloat16)


def add_pair(features_all, piece, previous):
    target_piece = blend(piece, previous)
    online_sum = jnp.dot(features_all, piece, preferred_element_type=jnp.float32)
    target_sum = jnp.dot(features_all, target_piece, preferred_element_type=jnp.float32)
    return (online_sum, target_sum)


def local(
    hidden_states, gate_online, up_online, down_online, gate_previous, up_previous, down_previous
):
    features_all = lax.all_gather(hidden_states, "mp", axis=1, tiled=True)
    gate_o, gate_t = add_pair(
        features_all, lax.all_gather(gate_online, "dp", axis=0, tiled=True), gate_previous
    )
    up_o, up_t = add_pair(
        features_all, lax.all_gather(up_online, "dp", axis=0, tiled=True), up_previous
    )
    inner_o = (jax.nn.silu(gate_o) * up_o).astype(jnp.bfloat16)
    inner_t = (jax.nn.silu(gate_t) * up_t).astype(jnp.bfloat16)
    piece = lax.all_gather(down_online, "dp", axis=1, tiled=True)
    target_piece = blend(piece, down_previous)
    online_part = jnp.dot(inner_o, piece, preferred_element_type=jnp.float32)
    target_part = jnp.dot(inner_t, target_piece, preferred_element_type=jnp.float32)
    terms = jnp.stack([online_part, target_part], axis=0)
    summed = lax.psum_scatter(terms, "mp", scatter_dimension=2, tiled=True)
    result = summed.astype(jnp.bfloat16)
    return (result[0], result[1])


def solution(mesh):
    in_specs = (
        P("dp", "mp"),
        P("dp", "mp"),
        P("dp", "mp"),
        P("mp", "dp"),
        P(None, "mp"),
        P(None, "mp"),
        P("mp", None),
    )
    out_specs = (P("dp", "mp"), P("dp", "mp"))
    return jax.shard_map(local, mesh=mesh, in_specs=in_specs, out_specs=out_specs, check_vma=False)
```

profile of v0, /device:TPU:1, one launch (start us, length us, event | category | flops | bytes accessed | tf_op | source)
XLA Modules:
  0.0 729.1 jit_solution(7389197562212726520)
XLA Ops:
  7.2 0.0 all-gather.5.cloned.1.call-start
  7.2 0.7 all-gather.5.cloned.1.call-update
  7.9 0.0 all-gather.7.cloned.1.call-start
  7.9 0.7 all-gather.7.cloned.1.call-update
  8.6 0.0 all-gather.9.cloned.1.call-start
  8.7 0.7 all-gather.9.cloned.1.call-update
  9.4 0.0 all-gather.11.cloned.1.call-start
  9.4 0.5 all-gather.11.cloned.1.call-update
  10.0 0.0 reduce-scatter.2.cloned.1.call-start
  10.0 60.8 %all-gather.5.cloned.1.call-done = bf16[512,4096]{1,0:T(8,128)(2,1)} async-done(((bf16[512,256]{1,0:T(8,128)(2,1)}), bf16[512,4096]{1,0:T(8,128)(2,1)}) %all-gather.5.cloned.1.call-update) | async-done | bytes 4194320 | tf_op jit(solution)/shard_map/all_gather | solution.py:25
  70.8 147.5 %all-gather.7.cloned.1.call-done = bf16[4096,896]{1,0:T(8,128)(2,1)} async-done(((bf16[512,896]{1,0:T(8,128)(2,1)}), bf16[4096,896]{1,0:T(8,128)(2,1)}) %all-gather.7.cloned.1.call-update) | async-done | bytes 7340048 | tf_op jit(solution)/shard_map/all_gather | solution.py:27
  218.3 10.2 %fusion.22 = f32[512,896]{1,0:T(8,128)} fusion(bf16[512,4096]{1,0:T(8,128)(2,1)} %all-gather.5.cloned.1.call-done, bf16[4096,896]{1,0:T(8,128)(2,1)} %all-gather.7.cloned.1.call-done), kind=kOutput, calls=%fused_computation.31 | convolution fusion | flops 3758096384 | bytes 13369344 | tf_op jit(solution)/shard_map/dot_general | solution.py:17
  228.5 0.0 copy-done
  228.5 0.0 copy-done.1
  228.5 7.9 %fusion = f32[896,512]{0,1:T(8,128)S(1)} fusion(bf16[512,4096]{1,0:T(8,128)(2,1)S(1)} %copy-done.1, bf16[4096,896]{1,0:T(8,128)(2,1)} %param.11, bf16[4096,896]{1,0:T(8,128)(2,1)S(1)} %copy-done), kind=kOutput, calls=%fused_computation.4 | convolution fusion | flops 3780116480 | bytes 20709376 | tf_op jit(solution)/shard_map/dot_general | solution.py:18
  236.5 133.2 %all-gather.9.cloned.1.call-done = bf16[4096,896]{1,0:T(8,128)(2,1)} async-done(((bf16[512,896]{1,0:T(8,128)(2,1)}), bf16[4096,896]{1,0:T(8,128)(2,1)}) %all-gather.9.cloned.1.call-update) | async-done | bytes 7340048 | tf_op jit(solution)/shard_map/all_gather | solution.py:30
  369.7 151.2 %all-gather.11.cloned.1.call-done = bf16[896,4096]{1,0:T(8,128)(2,1)} async-done(((bf16[896,512]{1,0:T(8,128)(2,1)}), bf16[896,4096]{1,0:T(8,128)(2,1)}) %all-gather.11.cloned.1.call-update) | async-done | bytes 7340048 | tf_op jit(solution)/shard_map/all_gather | solution.py:34
  520.9 17.2 %convolution_bitcast_fusion = f32[1,512,4096]{2,1,0:T(8,128)} fusion(bf16[896,4096]{1,0:T(8,128)(2,1)} %all-gather.11.cloned.1.call-done, f32[512,896]{1,0:T(8,128)} %fusion.22, bf16[512,4096]{1,0:T(8,128)(2,1)} %all-gather.5.cloned.1.call-done, bf16[4096,896]{1,0:T(8,128)(2,1)} %all-gather.9.cloned.1.call-done), kind=kOutput, calls=%fused_computation.14 | convolution fusion | flops 7518945280 | bytes 29097984 | tf_op jit(solution)/shard_map/dot_general | solution.py:36
  538.2 22.9 %fusion.9 = f32[1,512,4096]{2,1,0:T(8,128)} fusion(bf16[896,4096]{1,0:T(8,128)(2,1)} %param.13, bf16[896,4096]{1,0:T(8,128)(2,1)} %all-gather.11.cloned.1.call-done, f32[896,512]{0,1:T(8,128)S(1)} %fusion, bf16[512,4096]{1,0:T(8,128)(2,1)} %all-gather.5.cloned.1.call-done, bf16[4096,896]{1,0:T(8,128)(2,1)} %param.12, ...), kind=kOutput, calls=%fused_computation.13 | convolution fusion | flops 7562985472 | bytes 43778048 | tf_op jit(solution)/shard_map/dot_general | solution.py:37
  561.0 11.6 %pad_maximum_fusion = f32[2,512,4096]{2,1,0:T(8,128)} fusion(f32[1,512,4096]{2,1,0:T(8,128)} %fusion.9, f32[1,512,4096]{2,1,0:T(8,128)} %convolution_bitcast_fusion), kind=kLoop, calls=%fused_computation | loop fusion | flops 4194304 | bytes 33554432 | tf_op jit(solution)/shard_map/stack | solution.py:38
  572.6 0.0 reduce-scatter.2.cloned.1.call-update
  572.6 147.9 %reduce-scatter.2.cloned.1.call-done = f32[2,512,256]{2,1,0:T(8,128)} async-done(((f32[2,512,4096]{2,1,0:T(8,128)}), f32[2,512,256]{2,1,0:T(8,128)}) %reduce-scatter.2.cloned.1.call-update) | async-done | bytes 1048592 | tf_op jit(solution)/shard_map/reduce_scatter | solution.py:39
  720.5 1.3 convert_element_type.47
  721.8 0.8 slice_bitcast_fusion
  (2 shorter events, 0.0 us)
Async XLA Ops:
  7.2 63.6 %all-gather.5.cloned.1.call-start = ((), (), s32[]{:S(2)}) async-start(), calls=%async_computation.1 | async-start | bytes 4456448 | tf_op jit(solution)/shard_map/all_gather | solution.py:25
  7.9 210.4 %all-gather.7.cloned.1.call-start = ((), (), s32[]{:S(2)}) async-start(), calls=%async_computation.2 | async-start | bytes 8257536 | tf_op jit(solution)/shard_map/all_gather | solution.py:27
  8.6 361.0 %all-gather.9.cloned.1.call-start = ((), (), s32[]{:S(2)}) async-start(), calls=%async_computation.3 | async-start | bytes 8257536 | tf_op jit(solution)/shard_map/all_gather | solution.py:30
  9.4 511.5 %all-gather.11.cloned.1.call-start = ((), (), s32[]{:S(2)}) async-start(), calls=%async_computation.4 | async-start | bytes 8257536 | tf_op jit(solution)/shard_map/all_gather | solution.py:34
  10.0 710.6 %reduce-scatter.2.cloned.1.call-start = ((), (), s32[]{:S(2)}) async-start(), calls=%async_computation.5 | async-start | bytes 17825792 | tf_op jit(solution)/shard_map/reduce_scatter | solution.py:39
  218.3 10.2 %copy-start = (bf16[4096,896]{1,0:T(8,128)(2,1)S(1)}, bf16[4096,896]{1,0:T(8,128)(2,1)}, u32[]{:S(2)}) copy-start(bf16[4096,896]{1,0:T(8,128)(2,1)} %all-gather.7.cloned.1.call-done) | copy-start | bytes 22020100
  218.3 10.2 %copy-start.1 = (bf16[512,4096]{1,0:T(8,128)(2,1)S(1)}, bf16[512,4096]{1,0:T(8,128)(2,1)}, u32[]{:S(2)}) copy-start(bf16[512,4096]{1,0:T(8,128)(2,1)} %all-gather.5.cloned.1.call-done) | copy-start | bytes 12582916
Sparse Core Ops, SparseCore 0:
  10.3 60.4 all-gather.4
  72.4 145.8 all-gather.6
  220.0 149.6 all-gather.8
  371.2 149.6 all-gather.10
  572.7 147.7 reduce-scatter.1
where the time goes:
time: 729 us
  waiting for transfers between devices  643 us (88%)
  matrix products  58.3 us (8%)
  between operations  13.8 us (2%)
  other arithmetic  12.8 us (2%)
    all_gather x1, waiting for transfers between devices, local(): piece = lax.all_gather(down_online, 'dp', axis=1, tiled=True)  151 us
    reduce_scatter x1, waiting for transfers between devices, local(): summed = lax.psum_scatter(terms, 'mp', scatter_dimension=2, tiled=True)  148 us
    all_gather x1, waiting for transfers between devices, local(): lax.all_gather(gate_online, 'dp', axis=0, tiled=True)  148 us
    all_gather x1, waiting for transfers between devices, local(): lax.all_gather(up_online, 'dp', axis=0, tiled=True)  133 us
    all_gather x1, waiting for transfers between devices, local(): features_all = lax.all_gather(hidden_states, 'mp', axis=1, tiled=True)  60.8 us
    dot_general x1, matrix products, local(): jnp.dot(inner_t, target_piece, preferred_element_type=jnp.float32)  22.9 us
    dot_general x1, matrix products, local(): online_part = jnp.dot(inner_o, piece, preferred_element_type=jnp.float32)  17.2 us
  transfers between devices with their start and end apart: 5, of which 5 were waited for; matrix products, arithmetic and copies ran while one was open for 2% of the time, Pallas kernels for 0%

commit v1 on v0

--- a/solution.py
+++ b/solution.py
@@ -27,7 +27,11 @@
         features_all, lax.all_gather(gate_online, "dp", axis=0, tiled=True), gate_previous
     )
     up_o, up_t = add_pair(
-        features_all, lax.all_gather(up_online, "dp", axis=0, tiled=True), up_previous
+        features_all,
+        jnp.concatenate(
+            lax.all_to_all(jnp.stack([up_online] * lax.axis_size("dp")), "dp", 0, 0), axis=0
+        ),
+        up_previous,
     )
     inner_o = (jax.nn.silu(gate_o) * up_o).astype(jnp.bfloat16)
     inner_t = (jax.nn.silu(gate_t) * up_t).astype(jnp.bfloat16)

time: 729 us -> 616 us (0.84)
  waiting for transfers between devices: 643 us -> 518 us
    all_gather x1 -> x0, waiting for transfers between devices: 133 us -> none  [local(): lax.all_gather(up_online, 'dp', axis=0, tiled=True)]
    all_gather x1, waiting for transfers between devices: 148 us -> 170 us  [local(): lax.all_gather(gate_online, 'dp', axis=0, tiled=True)]
    all_gather x1, waiting for transfers between devices: 151 us -> 134 us  [local(): piece = lax.all_gather(down_online, 'dp', axis=1, tiled=True)]
  transfers between devices with their start and end apart: 5 -> 5, of which waited for: 5 -> 4; matrix products, arithmetic and copies ran while one was open for 2% -> 4% of each run, Pallas kernels for 0% -> 0%
where the time goes in v1:
time: 616 us; the launch traced here: 615 us
  waiting for transfers between devices  518 us (84%)
  matrix products  58.3 us (9%)
  between operations  13.8 us (2%)
  other arithmetic  12.8 us (2%)
    all_gather x1, waiting for transfers between devices, local(): lax.all_gather(gate_online, 'dp', axis=0, tiled=True)  170 us
    reduce_scatter x1, waiting for transfers between devices, local(): summed = lax.psum_scatter(terms, 'mp', scatter_dimension=2, tiled=True)  148 us
    all_gather x1, waiting for transfers between devices, local(): piece = lax.all_gather(down_online, 'dp', axis=1, tiled=True)  134 us
    all_gather x1, waiting for transfers between devices, local(): features_all = lax.all_gather(hidden_states, 'mp', axis=1, tiled=True)  64.9 us
    dot_general x1, matrix products, local(): jnp.dot(inner_t, target_piece, preferred_element_type=jnp.float32)  22.9 us
    dot_general x1, matrix products, local(): online_part = jnp.dot(inner_o, piece, preferred_element_type=jnp.float32)  17.2 us
  transfers between devices with their start and end apart: 5, of which 4 were waited for; matrix products, arithmetic and copies ran while one was open for 4% of the time, Pallas kernels for 0%

profile of v1, /device:TPU:1, one launch (start us, length us, event | category | flops | bytes accessed | tf_op | source)
XLA Modules:
  0.0 615.3 jit_solution(2265880455330164687)
XLA Ops:
  7.2 0.0 all-gather.4.cloned.1.call-start
  7.2 0.7 all-gather.4.cloned.1.call-update
  7.9 0.0 all-gather.6.cloned.1.call-start
  7.9 0.7 all-gather.6.cloned.1.call-update
  8.6 0.0 all-gather.8.cloned.1.call-start
  8.7 0.7 all-gather.8.cloned.1.call-update
  9.4 5.0 stack.8
  14.4 5.9 all-to-all-start
  20.4 0.0 reduce-scatter.2.cloned.1.call-start
  20.4 64.9 %all-gather.4.cloned.1.call-done = bf16[512,4096]{1,0:T(8,128)(2,1)} async-done(((bf16[512,256]{1,0:T(8,128)(2,1)}), bf16[512,4096]{1,0:T(8,128)(2,1)}) %all-gather.4.cloned.1.call-update) | async-done | bytes 4194320 | tf_op jit(solution)/shard_map/all_gather | solution.py:25
  85.3 169.6 %all-gather.6.cloned.1.call-done = bf16[4096,896]{1,0:T(8,128)(2,1)} async-done(((bf16[512,896]{1,0:T(8,128)(2,1)}), bf16[4096,896]{1,0:T(8,128)(2,1)}) %all-gather.6.cloned.1.call-update) | async-done | bytes 7340048 | tf_op jit(solution)/shard_map/all_gather | solution.py:27
  255.0 10.2 %fusion.22 = f32[512,896]{1,0:T(8,128)} fusion(bf16[512,4096]{1,0:T(8,128)(2,1)} %all-gather.4.cloned.1.call-done, bf16[4096,896]{1,0:T(8,128)(2,1)} %all-gather.6.cloned.1.call-done), kind=kOutput, calls=%fused_computation.31 | convolution fusion | flops 3758096384 | bytes 13369344 | tf_op jit(solution)/shard_map/dot_general | solution.py:17
  265.2 0.0 copy-done
  265.2 0.0 copy-done.1
  265.2 7.9 %fusion = f32[896,512]{0,1:T(8,128)S(1)} fusion(bf16[512,4096]{1,0:T(8,128)(2,1)S(1)} %copy-done.1, bf16[4096,896]{1,0:T(8,128)(2,1)} %param.11, bf16[4096,896]{1,0:T(8,128)(2,1)S(1)} %copy-done), kind=kOutput, calls=%fused_computation.4 | convolution fusion | flops 3780116480 | bytes 20709376 | tf_op jit(solution)/shard_map/dot_general | solution.py:18
  273.2 0.0 all-to-all-done
  273.2 133.5 %all-gather.8.cloned.1.call-done = bf16[896,4096]{1,0:T(8,128)(2,1)} async-done(((bf16[896,512]{1,0:T(8,128)(2,1)}), bf16[896,4096]{1,0:T(8,128)(2,1)}) %all-gather.8.cloned.1.call-update) | async-done | bytes 7340048 | tf_op jit(solution)/shard_map/all_gather | solution.py:38
  406.7 17.2 %convolution_bitcast_fusion = f32[1,512,4096]{2,1,0:T(8,128)} fusion(bf16[896,4096]{1,0:T(8,128)(2,1)} %all-gather.8.cloned.1.call-done, f32[512,896]{1,0:T(8,128)} %fusion.22, bf16[512,4096]{1,0:T(8,128)(2,1)} %all-gather.4.cloned.1.call-done, bf16[4096,896]{1,0:T(8,128)(2,1)} %bitcast), kind=kOutput, calls=%fused_computation.14 | convolution fusion | flops 7518945280 | bytes 29097984 | tf_op jit(solution)/shard_map/dot_general | solution.py:40
  424.0 22.9 %fusion.9 = f32[1,512,4096]{2,1,0:T(8,128)} fusion(bf16[896,4096]{1,0:T(8,128)(2,1)} %param.13, bf16[896,4096]{1,0:T(8,128)(2,1)} %all-gather.8.cloned.1.call-done, f32[896,512]{0,1:T(8,128)S(1)} %fusion, bf16[512,4096]{1,0:T(8,128)(2,1)} %all-gather.4.cloned.1.call-done, bf16[4096,896]{1,0:T(8,128)(2,1)} %param.12, bf16[4096,896]{1,0:T(8,128)(2,1)} %bitcast), kind=kOutput, calls=%fused_computation.13 | convolution fusion | flops 7562985472 | bytes 43778048 | tf_op jit(solution)/shard_map/dot_general | solution.py:41
  446.8 11.6 %pad_maximum_fusion = f32[2,512,4096]{2,1,0:T(8,128)} fusion(f32[1,512,4096]{2,1,0:T(8,128)} %fusion.9, f32[1,512,4096]{2,1,0:T(8,128)} %convolution_bitcast_fusion), kind=kLoop, calls=%fused_computation | loop fusion | flops 4194304 | bytes 33554432 | tf_op jit(solution)/shard_map/stack | solution.py:42
  458.4 0.0 reduce-scatter.2.cloned.1.call-update
  458.4 148.3 %reduce-scatter.2.cloned.1.call-done = f32[2,512,256]{2,1,0:T(8,128)} async-done(((f32[2,512,4096]{2,1,0:T(8,128)}), f32[2,512,256]{2,1,0:T(8,128)}) %reduce-scatter.2.cloned.1.call-update) | async-done | bytes 1048592 | tf_op jit(solution)/shard_map/reduce_scatter | solution.py:43
  606.7 1.3 convert_element_type.47
  608.0 0.8 slice_bitcast_fusion
  (2 shorter events, 0.0 us)
Async XLA Ops:
  7.2 78.2 %all-gather.4.cloned.1.call-start = ((), (), s32[]{:S(2)}) async-start(), calls=%async_computation.2 | async-start | bytes 4456448 | tf_op jit(solution)/shard_map/all_gather | solution.py:25
  7.9 247.1 %all-gather.6.cloned.1.call-start = ((), (), s32[]{:S(2)}) async-start(), calls=%async_computation.3 | async-start | bytes 8257536 | tf_op jit(solution)/shard_map/all_gather | solution.py:27
  8.6 398.1 %all-gather.8.cloned.1.call-start = ((), (), s32[]{:S(2)}) async-start(), calls=%async_computation.4 | async-start | bytes 8257536 | tf_op jit(solution)/shard_map/all_gather | solution.py:38
  14.4 258.7 %all-to-all-start = ((bf16[8,512,896]{2,1,0:T(8,128)(2,1)}), bf16[8,512,896]{2,1,0:T(8,128)(2,1)}, u32[]{:S(2)}, u32[]{:S(2)}) async-start(bf16[8,512,896]{2,1,0:T(8,128)(2,1)} %stack.8), calls=%async_computation | async-start | bytes 14680064 | tf_op jit(solution)/shard_map/all_to_all | solution.py:32
  20.4 586.3 %reduce-scatter.2.cloned.1.call-start = ((), (), s32[]{:S(2)}) async-start(), calls=%async_computation.5 | async-start | bytes 17825792 | tf_op jit(solution)/shard_map/reduce_scatter | solution.py:43
  255.0 10.2 %copy-start = (bf16[4096,896]{1,0:T(8,128)(2,1)S(1)}, bf16[4096,896]{1,0:T(8,128)(2,1)}, u32[]{:S(2)}) copy-start(bf16[4096,896]{1,0:T(8,128)(2,1)} %all-gather.6.cloned.1.call-done) | copy-start | bytes 22020100
  255.0 10.2 %copy-start.1 = (bf16[512,4096]{1,0:T(8,128)(2,1)S(1)}, bf16[512,4096]{1,0:T(8,128)(2,1)}, u32[]{:S(2)}) copy-start(bf16[512,4096]{1,0:T(8,128)(2,1)} %all-gather.4.cloned.1.call-done) | copy-start | bytes 12582916
Sparse Core Ops, SparseCore 0:
  10.3 75.0 all-gather.3
  87.0 167.9 all-gather.5
  256.6 150.0 all-gather.7
  458.5 148.1 reduce-scatter.1
